TPU v7x, 32 devices: a whole 2x2x4 slice. The times are simulated.
32 devices in a mesh: station: 8 (over y, x, core), tm: 4 (over z).
Axes of the slice: x: 2, y: 2, z: 4, core: 2. Of those that a mesh axis runs over, the one named last changes fastest.
Arguments:
- samples: bfloat16 [64, 256, 2048], P('tm', 'station'), may hold values from -6 to 6
- history: bfloat16 [15, 256, 2048], P(None, 'station'), may hold values from -6 to 6
- taps: float32 [16, 2048], replicated, may hold values from -0.03125 to 0.03125
Outputs:
- visibility: float32 [1024, 2, 256, 256], P(('station', 'tm'))
- beam_power: float32 [64, 1024], P('tm', 'station')
All inputs are finite; a program needn't handle non-finite values.
Results may differ from a plain program's by a relative error of at most 0.0095.
Values may be sent and summed in bfloat16 or wider, within the bound.
A program may use at most 128 MiB of HBM per device.

v0:
```python
import math
import jax
import jax.numpy as jnp
from jax import lax
from jax.sharding import PartitionSpec as P


def passed_along(block, axis, distance):
    devices = range(lax.axis_size(axis))
    route = [(i - distance, i) for i in devices if i - distance in devices]
    return lax.ppermute(block, axis, route)


def dft_parts(frame_len, channels):
    sample_index = jnp.arange(frame_len, dtype=jnp.int32)
    channel_index = jnp.arange(channels, dtype=jnp.int32)
    phases = sample_index[:, None] * channel_index[None, :] % frame_len
    angles = phases.astype(jnp.float32) * (2.0 * math.pi / frame_len)
    return (jnp.cos(angles).astype(jnp.bfloat16), (-jnp.sin(angles)).astype(jnp.bfloat16))


def filter_frames(extended, taps, frames_out):
    span_taps = taps.shape[0]
    running = jnp.zeros((frames_out,) + extended.shape[1:], jnp.float32)
    for tap_index in range(span_taps):
        offset = span_taps - 1 - tap_index
        running = running + taps[tap_index][None, None, :] * extended[
            offset : offset + frames_out
        ].astype(jnp.float32)
    return jnp.swapaxes(running, 0, 1).astype(jnp.bfloat16)


def power_of(grouped):
    values = grouped.astype(jnp.float32)
    return jnp.sum(values * values, axis=(-3, -2)) * (1.0 / grouped.shape[-3])


def flat_pair(piece):
    chan_count, input_count, pair_count, frame_count = piece.shape
    flat = piece.reshape(chan_count, input_count, pair_count * frame_count)
    rotated = jnp.concatenate([-piece[:, :, 1:2], piece[:, :, 0:1]], axis=2)
    return (flat, rotated.reshape(chan_count, input_count, pair_count * frame_count))


def correlate(piece, norm_scale):
    flat, rotated = flat_pair(piece)
    real_part = (
        jnp.einsum("cak,cbk->cab", flat, flat, preferred_element_type=jnp.float32) * norm_scale
    )
    imag_part = (
        jnp.einsum("cak,cbk->cab", rotated, flat, preferred_element_type=jnp.float32) * norm_scale
    )
    return (real_part, imag_part)


def body(samples, history, taps):
    frames_dev = samples.shape[0]
    frame_len = samples.shape[2]
    span_taps = taps.shape[0]
    cos_part, sin_part = dft_parts(frame_len, frame_len // 2)
    tail_block = samples[frames_dev - (span_taps - 1) :]
    prior_frames = passed_along(tail_block, "tm", 1)
    prior_frames = jnp.where(lax.axis_index("tm") == 0, history, prior_frames)
    extended = jnp.concatenate([prior_frames, samples], axis=0)
    weighted = filter_frames(extended, taps, frames_dev)
    real_spec = jnp.einsum("nc,atn->cat", cos_part, weighted, preferred_element_type=jnp.float32)
    imag_spec = jnp.einsum("nc,atn->cat", sin_part, weighted, preferred_element_type=jnp.float32)
    spectra = jnp.stack([real_spec, imag_spec], axis=2).astype(jnp.bfloat16)
    time_groups = lax.axis_size("tm")
    norm_scale = 1.0 / (frames_dev * time_groups)
    gathered = lax.all_to_all(
        lax.all_to_all(spectra[None], "station", split_axis=1, concat_axis=2, tiled=True),
        "tm",
        split_axis=1,
        concat_axis=0,
        tiled=True,
    )
    own_channels = gathered.shape[1]
    inputs = gathered.shape[2]
    power_own = power_of(gathered)
    power_back = lax.all_to_all(power_own, "tm", split_axis=0, concat_axis=1, tiled=True)
    power_rows = jnp.transpose(power_back[0])

    def accumulate(block_index, running):
        time_piece = lax.dynamic_index_in_dim(gathered, block_index, 0, keepdims=False)
        real_part, imag_part = correlate(time_piece, norm_scale)
        partial_value = jnp.stack([real_part, imag_part], axis=1).astype(jnp.bfloat16)
        partial_value = lax.optimization_barrier(partial_value)
        return running + partial_value.astype(jnp.float32)

    initial_sum = jnp.zeros((own_channels, 2, inputs, inputs), jnp.float32)
    visibility = lax.fori_loop(0, time_groups, accumulate, initial_sum)
    return (visibility, power_rows)


def solution(mesh):
    return jax.shard_map(
        body,
        mesh=mesh,
        in_specs=(P("tm", "station", None), P(None, "station", None), P()),
        out_specs=(P(("station", "tm"), None, None, None), P("tm", "station")),
        check_vma=False,
    )
```

profile of v0, /device:TPU:0, one launch (start us, length us, event | category | flops | bytes accessed | tf_op | source)
XLA Modules:
  0.0 371.6 jit_solution(146463902237839219)
XLA Ops:
  0.6 3.2 slice.112
  3.8 6.2 %collective-permute-start = (bf16[15,32,2048]{2,1,0:T(8,128)(2,1)}, bf16[15,32,2048]{2,1,0:T(8,128)(2,1)}, u32[]{:S(2)}, u32[]{:S(2)}) collective-permute-start(bf16[15,32,2048]{2,1,0:T(8,128)(2,1)} %slice.112), channel_id=1, source_target_pairs={{0,1},{1,2},{2,3},{4,5},{5,6},{6,7},{8,9},{9,10},{10,11},{12,13},{... | collective-permute-start | bytes 5898248 | tf_op jit(solution)/shard_map/ppermute | solution.py:11
  10.1 1.6 fusion.60
  11.7 39.5 %collective-permute-done = bf16[15,32,2048]{2,1,0:T(8,128)(2,1)} collective-permute-done((bf16[15,32,2048]{2,1,0:T(8,128)(2,1)}, bf16[15,32,2048]{2,1,0:T(8,128)(2,1)}, u32[]{:S(2)}, u32[]{:S(2)}) %collective-permute-start) | collective-permute-done | bytes 1966112 | tf_op jit(solution)/shard_map/ppermute | solution.py:11
  51.1 1.8 broadcast_select_fusion
  52.9 9.5 %add_convert_fusion = bf16[16,32,2048]{2,1,0:T(8,128)(2,1)S(1)} fusion(bf16[16,32,2048]{2,1,0:T(8,128)(2,1)S(1)} %copy-done, bf16[15,32,2048]{2,1,0:T(8,128)(2,1)S(1)} %broadcast_select_fusion, f32[2048]{0:T(1024)S(1)} %bitcast.116, f32[2048]{0:T(1024)S(1)} %bitcast.117, f32[2048]{0:T(1024)S(1)} %bitcast.103, f32[2048]{0:T(1024)S(1)} %bitcast.104, ...), kind=kLoop, calls=%fused_computation.53 | loop fusion | flops 66060288 | bytes 6291456 | tf_op jit(solution)/shard_map/convert_element_type | solution.py:30
  62.4 31.8 %fusion.42 = bf16[1,1024,32,1,16]{1,2,4,3,0:T(8,128)(2,1)S(1)} fusion(bf16[16,32,2048]{2,1,0:T(8,128)(2,1)S(1)} %add_convert_fusion), kind=kOutput, calls=%fused_computation.75 | convolution fusion | flops 2179465216 | bytes 3145728 | tf_op jit(solution)/shard_map/nc,atn->cat/dot_general | solution.py:66
  94.2 32.5 %fusion.47 = bf16[1,1024,32,1,16]{1,2,4,3,0:T(8,128)(2,1)S(1)} fusion(bf16[16,32,2048]{2,1,0:T(8,128)(2,1)S(1)} %add_convert_fusion), kind=kOutput, calls=%fused_computation.76 | convolution fusion | flops 2181562368 | bytes 3145728 | tf_op jit(solution)/shard_map/nc,atn->cat/dot_general | solution.py:67
  126.8 12.1 %copy.33 = bf16[1,1024,32,2,16]{2,4,3,0,1:T(8,128)(2,1)} copy(bf16[1,1024,32,2,16]{1,2,4,3,0:T(8,128)(2,1)S(1)} %pad_maximum_fusion.3) | data formatting | bytes 4194304 | tf_op jit(solution)/shard_map/stack | solution.py:68
  138.9 10.1 %reshape.82 = bf16[8,2,65536]{2,1,0:T(2,128)(2,1)S(1)} reshape(bf16[1024,1,2,16,32]{4,3,2,1,0:T(8,128)(2,1)} %bitcast.96) | data formatting | bytes 4194304
  149.1 30.2 %all_to_all.39 = bf16[8,2,65536]{2,1,0:T(2,128)(2,1)} all-to-all(bf16[8,2,65536]{2,1,0:T(2,128)(2,1)S(1)} %reshape.82), channel_id=1, replica_groups=mesh['station'=8,'tm'=4] {'station'}, dimensions={0} | all-to-all | bytes 4194304 | tf_op jit(solution)/shard_map/all_to_all | solution.py:72
  179.3 8.6 %reshape.83 = bf16[1024,1,2,16,32]{4,3,2,1,0:T(8,128)(2,1)} reshape(bf16[8,2,65536]{2,1,0:T(2,128)(2,1)} %all_to_all.39) | data formatting | bytes 4194304
  187.9 9.3 %copy.42 = bf16[1,8,128,32,2,16]{2,1,5,4,3,0:T(8,128)(2,1)S(1)} copy(bf16[1,8,128,32,2,16]{3,5,4,2,1,0:T(8,128)(2,1)} %bitcast.97) | data formatting | bytes 4194304 | tf_op jit(solution)/shard_map/all_to_all | solution.py:72
  197.2 1.7 copy.35
  198.9 4.9 %copy.36 = bf16[1,128,256,2,16]{2,4,3,0,1:T(8,128)(2,1)} copy(bf16[1,128,256,2,16]{1,4,3,2,0:T(8,128)(2,1)} %bitcast.99) | data formatting | bytes 4194304 | tf_op jit(solution)/shard_map/all_to_all | solution.py:72
  203.8 5.8 %all-to-all-start.1 = ((bf16[1,128,256,2,16]{2,4,3,0,1:T(8,128)(2,1)}), bf16[1,128,256,2,16]{2,4,3,0,1:T(8,128)(2,1)S(1)}, u32[]{:S(2)}, u32[]{:S(2)}) async-start(bf16[1,128,256,2,16]{2,4,3,0,1:T(8,128)(2,1)} %copy.36), calls=%async_computation.1 | async-start | bytes 4194304 | tf_op jit(solution)/shard_map/all_to_all | solution.py:71
  209.6 47.5 %all-to-all-done.1 = bf16[1,128,256,2,16]{2,4,3,0,1:T(8,128)(2,1)S(1)} async-done(((bf16[1,128,256,2,16]{2,4,3,0,1:T(8,128)(2,1)}), bf16[1,128,256,2,16]{2,4,3,0,1:T(8,128)(2,1)S(1)}, u32[]{:S(2)}, u32[]{:S(2)}) %all-to-all-start.1) | async-done | bytes 2097184 | tf_op jit(solution)/shard_map/all_to_all | solution.py:71
  258.4 3.2 all-to-all-start.2
  261.7 96.2 %while.14 = (s32[]{:T(128)}, f32[32,2,256,256]{3,2,0,1:T(8,128)}, bf16[4,32,256,2,16]{2,4,3,1,0:T(8,128)(2,1)S(1)}, s32[]{:T(128)}, s32[]{:T(128)}) while((s32[]{:T(128)}, f32[32,2,256,256]{3,2,0,1:T(8,128)}, bf16[4,32,256,2,16]{2,4,3,1,0:T(8,128)(2,1)S(1)}, s32[]{:T(128)}, s32[]{:T(128)}) %tuple.65), condition=%wide.region_1.2_spmd.clone, body=%wide.region_0.1_spmd.clone.sunk | while | flops 293994496 | bytes 72876112 | solution.py:92
  263.2 3.2 fusion.79
  266.4 6.3 %pad_maximum_fusion.7 = bf16[32,2,256,256]{3,2,0,1:T(8,128)(2,1)} fusion(bf16[32,1,256,256]{3,2,0,1:T(8,128)(2,1)S(1)} %fusion.78, bf16[32,1,256,256]{3,2,0,1:T(8,128)(2,1)} %fusion.79), kind=kLoop, calls=%fused_computation.1.clone.1 | loop fusion | flops 4194304 | bytes 16777216 | tf_op jit(solution)/shard_map/while/body/eval_jaxpr/stack | solution.py:87
  272.8 9.9 %select_add_fusion.2 = f32[32,2,256,256]{3,2,0,1:T(8,128)} fusion(f32[32,2,256,256]{3,2,0,1:T(8,128)} %get-tuple-element.149, bf16[32,2,256,256]{3,2,0,1:T(8,128)(2,1)} %pad_maximum_fusion.7, pred[]{:T(512)S(6)} %compare.4), kind=kLoop, calls=%fused_computation.clone.1 | loop fusion | flops 12582912 | bytes 41943040 | tf_op jit(solution)/shard_map/while/body/eval_jaxpr/add | solution.py:89
  284.2 3.2 fusion.79
  287.5 6.3 %pad_maximum_fusion.7 = bf16[32,2,256,256]{3,2,0,1:T(8,128)(2,1)} fusion(bf16[32,1,256,256]{3,2,0,1:T(8,128)(2,1)S(1)} %fusion.78, bf16[32,1,256,256]{3,2,0,1:T(8,128)(2,1)} %fusion.79), kind=kLoop, calls=%fused_computation.1.clone.1 | loop fusion | flops 4194304 | bytes 16777216 | tf_op jit(solution)/shard_map/while/body/eval_jaxpr/stack | solution.py:87
  293.8 14.0 %select_add_fusion.2 = f32[32,2,256,256]{3,2,0,1:T(8,128)} fusion(f32[32,2,256,256]{3,2,0,1:T(8,128)} %get-tuple-element.149, bf16[32,2,256,256]{3,2,0,1:T(8,128)(2,1)} %pad_maximum_fusion.7, pred[]{:T(512)S(6)} %compare.4), kind=kLoop, calls=%fused_computation.clone.1 | loop fusion | flops 12582912 | bytes 41943040 | tf_op jit(solution)/shard_map/while/body/eval_jaxpr/add | solution.py:89
  309.3 3.2 fusion.79
  312.5 6.3 %pad_maximum_fusion.7 = bf16[32,2,256,256]{3,2,0,1:T(8,128)(2,1)} fusion(bf16[32,1,256,256]{3,2,0,1:T(8,128)(2,1)S(1)} %fusion.78, bf16[32,1,256,256]{3,2,0,1:T(8,128)(2,1)} %fusion.79), kind=kLoop, calls=%fused_computation.1.clone.1 | loop fusion | flops 4194304 | bytes 16777216 | tf_op jit(solution)/shard_map/while/body/eval_jaxpr/stack | solution.py:87
  318.9 14.0 %select_add_fusion.2 = f32[32,2,256,256]{3,2,0,1:T(8,128)} fusion(f32[32,2,256,256]{3,2,0,1:T(8,128)} %get-tuple-element.149, bf16[32,2,256,256]{3,2,0,1:T(8,128)(2,1)} %pad_maximum_fusion.7, pred[]{:T(512)S(6)} %compare.4), kind=kLoop, calls=%fused_computation.clone.1 | loop fusion | flops 12582912 | bytes 41943040 | tf_op jit(solution)/shard_map/while/body/eval_jaxpr/add | solution.py:89
  334.3 3.2 fusion.79
  337.6 6.3 %pad_maximum_fusion.7 = bf16[32,2,256,256]{3,2,0,1:T(8,128)(2,1)} fusion(bf16[32,1,256,256]{3,2,0,1:T(8,128)(2,1)S(1)} %fusion.78, bf16[32,1,256,256]{3,2,0,1:T(8,128)(2,1)} %fusion.79), kind=kLoop, calls=%fused_computation.1.clone.1 | loop fusion | flops 4194304 | bytes 16777216 | tf_op jit(solution)/shard_map/while/body/eval_jaxpr/stack | solution.py:87
  343.9 14.0 %select_add_fusion.2 = f32[32,2,256,256]{3,2,0,1:T(8,128)} fusion(f32[32,2,256,256]{3,2,0,1:T(8,128)} %get-tuple-element.149, bf16[32,2,256,256]{3,2,0,1:T(8,128)(2,1)} %pad_maximum_fusion.7, pred[]{:T(512)S(6)} %compare.4), kind=kLoop, calls=%fused_computation.clone.1 | loop fusion | flops 12582912 | bytes 41943040 | tf_op jit(solution)/shard_map/while/body/eval_jaxpr/add | solution.py:89
  357.9 11.7 %copy.41 = f32[32,2,256,256]{3,2,1,0:T(8,128)} copy(f32[32,2,256,256]{3,2,0,1:T(8,128)} %get-tuple-element.94) | data formatting | bytes 33554432
  (36 shorter events, 9.3 us)
Async XLA Ops:
  0.6 52.3 %copy-start = (bf16[16,32,2048]{2,1,0:T(8,128)(2,1)S(1)}, bf16[16,32,2048]{2,1,0:T(8,128)(2,1)}, u32[]{:S(2)}) copy-start(bf16[16,32,2048]{2,1,0:T(8,128)(2,1)} %param.5) | copy-start | bytes 6291460
  3.8 47.3 %collective-permute-start = (bf16[15,32,2048]{2,1,0:T(8,128)(2,1)}, bf16[15,32,2048]{2,1,0:T(8,128)(2,1)}, u32[]{:S(2)}, u32[]{:S(2)}) collective-permute-start(bf16[15,32,2048]{2,1,0:T(8,128)(2,1)} %slice.112), channel_id=1, source_target_pairs={{0,1},{1,2},{2,3},{4,5},{5,6},{6,7},{8,9},{9,10},{10,11},{12,13},{... | collective-permute-start | bytes 5898248 | tf_op jit(solution)/shard_map/ppermute | solution.py:11
  203.8 53.3 %all-to-all-start.1 = ((bf16[1,128,256,2,16]{2,4,3,0,1:T(8,128)(2,1)}), bf16[1,128,256,2,16]{2,4,3,0,1:T(8,128)(2,1)S(1)}, u32[]{:S(2)}, u32[]{:S(2)}) async-start(bf16[1,128,256,2,16]{2,4,3,0,1:T(8,128)(2,1)} %copy.36), calls=%async_computation.1 | async-start | bytes 4194304 | tf_op jit(solution)/shard_map/all_to_all | solution.py:71
  258.4 111.2 %all-to-all-start.2 = ((f32[4,1,512]{2,1,0:T(1,128)}), f32[4,1,512]{2,1,0:T(1,128)S(1)}, u32[]{:S(2)}, u32[]{:S(2)}) async-start(f32[4,1,512]{2,1,0:T(1,128)} %reshape.84), calls=%async_computation.2 | async-start | bytes 16384 | tf_op jit(solution)/shard_map/all_to_all | solution.py:81
where the time goes:
time: 373 us; the launch traced here: 372 us
  other arithmetic  90.2 us (24%)
  waiting for transfers between devices  87 us (23%)
  matrix products  82.4 us (22%)
  local copies, waits for them, and re-layouts  65.6 us (18%)
  blocking collectives  30.2 us (8%)
  starting transfers between devices  15.2 us (4%)
    add x4, other arithmetic, accumulate(): return running + partial_value.astype(jnp.float32)  51.9 us
    all_to_all x1, waiting for transfers between devices, body(): lax.all_to_all(lax.all_to_all(spectra[None], 'station', split_axis=1, con...  47.5 us
    ppermute x1, waiting for transfers between devices, passed_along(): return lax.ppermute(block, axis, route)  39.5 us
    dot_general x1, matrix products, body(): jnp.einsum('nc,atn->cat', sin_part, weighted, preferred_element_type=jnp....  32.5 us
    dot_general x1, matrix products, body(): jnp.einsum('nc,atn->cat', cos_part, weighted, preferred_element_type=jnp....  31.8 us
    unnamed x7, local copies, waits for them, and re-layouts  31.2 us
    all_to_all x1, blocking collectives, body(): lax.all_to_all(spectra[None], 'station', split_axis=1, concat_axis=2, til...  30.2 us
    another operation x4, other arithmetic, accumulate(): jnp.stack([real_part, imag_part], axis=1).astype(jnp.bfloat16)  25.4 us
  transfers between devices with their start and end apart: 3, of which 2 were waited for; matrix products, arithmetic and copies ran while one was open for 29% of the time, Pallas kernels for 0%

commit v1 on v0

--- a/solution.py
+++ b/solution.py
@@ -69,7 +69,15 @@
     time_groups = lax.axis_size("tm")
     norm_scale = 1.0 / (frames_dev * time_groups)
     gathered = lax.all_to_all(
-        lax.all_to_all(spectra[None], "station", split_axis=1, concat_axis=2, tiled=True),
+        jnp.concatenate(
+            lax.all_to_all(
+                jnp.stack(jnp.split(spectra[None], lax.axis_size("station"), axis=1)),
+                "station",
+                0,
+                0,
+            ),
+            axis=2,
+        ),
         "tm",
         split_axis=1,
         concat_axis=0,

time: 373 us -> 333 us (0.89)
  local copies, waits for them, and re-layouts: 65.6 us -> 26 us
    unnamed x7 -> x5, local copies, waits for them, and re-layouts: 31.2 us -> 12.4 us
    all_to_all x3 -> x0, local copies, waits for them, and re-layouts: 15.9 us -> none  [body(): lax.all_to_all(spectra[None], 'station', split_axis=1, concat_axis=2, til...]
    another operation x1 -> x0, local copies, waits for them, and re-layouts: 12.1 us -> none  [body(): spectra = jnp.stack([real_spec, imag_spec], axis=2).astype(jnp.bfloat16)]
    reshape x0 -> x2, local copies, waits for them, and re-layouts: none -> 7.05 us  [body(): jnp.concatenate(lax.all_to_all(jnp.stack(jnp.split(spectra[None], lax.axi...]
  transfers between devices with their start and end apart: 3 -> 3, of which waited for: 2 -> 2; matrix products, arithmetic and copies ran while one was open for 29% -> 33% of each run, Pallas kernels for 0% -> 0%
where the time goes in v1:
time: 333 us
  other arithmetic  90.6 us (27%)
  waiting for transfers between devices  87 us (26%)
  matrix products  82.4 us (25%)
  blocking collectives  30.1 us (9%)
  local copies, waits for them, and re-layouts  26 us (8%)
  starting transfers between devices  15.5 us (5%)
    add x4, other arithmetic, accumulate(): return running + partial_value.astype(jnp.float32)  51.9 us
    all_to_all x1, waiting for transfers between devices, body(): lax.all_to_all(jnp.concatenate(lax.all_to_all(jnp.stack(jnp.split(spectra...  47.5 us
    ppermute x1, waiting for transfers between devices, passed_along(): return lax.ppermute(block, axis, route)  39.5 us
    dot_general x1, matrix products, body(): jnp.einsum('nc,atn->cat', sin_part, weighted, preferred_element_type=jnp....  32.5 us
    dot_general x1, matrix products, body(): jnp.einsum('nc,atn->cat', cos_part, weighted, preferred_element_type=jnp....  31.8 us
    all_to_all x1, blocking collectives, body(): lax.all_to_all(jnp.stack(jnp.split(spectra[None], lax.axis_size('station'...  30.1 us
    another operation x4, other arithmetic, accumulate(): jnp.stack([real_part, imag_part], axis=1).astype(jnp.bfloat16)  25.4 us
    dot_general x4, matrix products, correlate(): jnp.einsum('cak,cbk->cab', flat, flat, preferred_element_type=jnp.float32)  13 us
  transfers between devices with their start and end apart: 3, of which 2 were waited for; matrix products, arithmetic and copies ran while one was open for 33% of the time, Pallas kernels for 0%

profile of v1, /device:TPU:0, one launch (start us, length us, event | category | flops | bytes accessed | tf_op | source)
XLA Modules:
  0.0 332.5 jit_solution(14042927272661791361)
XLA Ops:
  0.6 3.2 slice.112
  3.8 6.2 %collective-permute-start = (bf16[15,32,2048]{2,1,0:T(8,128)(2,1)}, bf16[15,32,2048]{2,1,0:T(8,128)(2,1)}, u32[]{:S(2)}, u32[]{:S(2)}) collective-permute-start(bf16[15,32,2048]{2,1,0:T(8,128)(2,1)} %slice.112), channel_id=1, source_target_pairs={{0,1},{1,2},{2,3},{4,5},{5,6},{6,7},{8,9},{9,10},{10,11},{12,13},{... | collective-permute-start | bytes 5898248 | tf_op jit(solution)/shard_map/ppermute | solution.py:11
  10.1 1.6 fusion.69
  11.7 39.5 %collective-permute-done = bf16[15,32,2048]{2,1,0:T(8,128)(2,1)} collective-permute-done((bf16[15,32,2048]{2,1,0:T(8,128)(2,1)}, bf16[15,32,2048]{2,1,0:T(8,128)(2,1)}, u32[]{:S(2)}, u32[]{:S(2)}) %collective-permute-start) | collective-permute-done | bytes 1966112 | tf_op jit(solution)/shard_map/ppermute | solution.py:11
  51.1 1.8 broadcast_select_fusion
  52.9 9.5 %add_convert_fusion = bf16[16,32,2048]{2,1,0:T(8,128)(2,1)S(1)} fusion(bf16[16,32,2048]{2,1,0:T(8,128)(2,1)S(1)} %copy-done, bf16[15,32,2048]{2,1,0:T(8,128)(2,1)S(1)} %broadcast_select_fusion, f32[2048]{0:T(1024)S(1)} %bitcast.129, f32[2048]{0:T(1024)S(1)} %bitcast.130, f32[2048]{0:T(1024)S(1)} %bitcast.116, f32[2048]{0:T(1024)S(1)} %bitcast.117, ...), kind=kLoop, calls=%fused_computation.53 | loop fusion | flops 66060288 | bytes 6291456 | tf_op jit(solution)/shard_map/convert_element_type | solution.py:30
  62.4 31.8 %fusion.42 = bf16[1,1024,32,1,16]{1,2,4,3,0:T(8,128)(2,1)S(1)} fusion(bf16[16,32,2048]{2,1,0:T(8,128)(2,1)S(1)} %add_convert_fusion), kind=kOutput, calls=%fused_computation.88 | convolution fusion | flops 2179465216 | bytes 3145728 | tf_op jit(solution)/shard_map/nc,atn->cat/dot_general | solution.py:66
  94.2 32.5 %fusion.47 = bf16[1,1024,32,1,16]{1,2,4,3,0:T(8,128)(2,1)S(1)} fusion(bf16[16,32,2048]{2,1,0:T(8,128)(2,1)S(1)} %add_convert_fusion), kind=kOutput, calls=%fused_computation.89 | convolution fusion | flops 2181562368 | bytes 3145728 | tf_op jit(solution)/shard_map/nc,atn->cat/dot_general | solution.py:67
  127.4 30.1 %all_to_all.26 = bf16[8,1,128,32,2,16]{2,3,5,4,1,0:T(8,128)(2,1)S(1)} all-to-all(bf16[8,1,128,32,2,16]{2,3,5,4,1,0:T(8,128)(2,1)S(1)} %fusion.60), channel_id=1, replica_groups=mesh['station'=8,'tm'=4] {'station'}, dimensions={0} | all-to-all | bytes 4194304 | tf_op jit(solution)/shard_map/all_to_all | solution.py:73
  157.5 2.1 copy.29
  159.6 4.9 %copy.30 = bf16[1,128,256,2,16]{2,4,3,0,1:T(8,128)(2,1)} copy(bf16[1,128,256,2,16]{1,4,3,2,0:T(8,128)(2,1)} %bitcast.112) | data formatting | bytes 4194304 | tf_op jit(solution)/shard_map/reshape | solution.py:72
  164.5 5.8 %all-to-all-start.1 = ((bf16[1,128,256,2,16]{2,4,3,0,1:T(8,128)(2,1)}), bf16[1,128,256,2,16]{2,4,3,0,1:T(8,128)(2,1)S(1)}, u32[]{:S(2)}, u32[]{:S(2)}) async-start(bf16[1,128,256,2,16]{2,4,3,0,1:T(8,128)(2,1)} %copy.30), calls=%async_computation.1 | async-start | bytes 4194304 | tf_op jit(solution)/shard_map/all_to_all | solution.py:71
  170.3 47.5 %all-to-all-done.1 = bf16[1,128,256,2,16]{2,4,3,0,1:T(8,128)(2,1)S(1)} async-done(((bf16[1,128,256,2,16]{2,4,3,0,1:T(8,128)(2,1)}), bf16[1,128,256,2,16]{2,4,3,0,1:T(8,128)(2,1)S(1)}, u32[]{:S(2)}, u32[]{:S(2)}) %all-to-all-start.1) | async-done | bytes 2097184 | tf_op jit(solution)/shard_map/all_to_all | solution.py:71
  219.2 3.5 %all-to-all-start.2 = ((f32[4,1,512]{2,1,0:T(1,128)}), f32[4,1,512]{2,1,0:T(1,128)S(1)}, u32[]{:S(2)}, u32[]{:S(2)}) async-start(f32[4,1,512]{2,1,0:T(1,128)} %reshape.90), calls=%async_computation.2 | async-start | bytes 16384 | tf_op jit(solution)/shard_map/all_to_all | solution.py:89
  222.6 96.2 %while.14 = (s32[]{:T(128)}, f32[32,2,256,256]{3,2,0,1:T(8,128)}, bf16[4,32,256,2,16]{2,4,3,1,0:T(8,128)(2,1)S(1)}, s32[]{:T(128)}, s32[]{:T(128)}) while((s32[]{:T(128)}, f32[32,2,256,256]{3,2,0,1:T(8,128)}, bf16[4,32,256,2,16]{2,4,3,1,0:T(8,128)(2,1)S(1)}, s32[]{:T(128)}, s32[]{:T(128)}) %tuple.65), condition=%wide.region_1.2_spmd.clone, body=%wide.region_0.1_spmd.clone.sunk | while | flops 293994496 | bytes 72876112 | solution.py:100
  222.9 1.3 fusion.87
  224.2 3.2 fusion.88
  227.4 6.3 %pad_maximum_fusion.7 = bf16[32,2,256,256]{3,2,0,1:T(8,128)(2,1)} fusion(bf16[32,1,256,256]{3,2,0,1:T(8,128)(2,1)S(1)} %fusion.87, bf16[32,1,256,256]{3,2,0,1:T(8,128)(2,1)} %fusion.88), kind=kLoop, calls=%fused_computation.1.clone.1 | loop fusion | flops 4194304 | bytes 16777216 | tf_op jit(solution)/shard_map/while/body/eval_jaxpr/stack | solution.py:95
  233.8 9.9 %select_add_fusion.2 = f32[32,2,256,256]{3,2,0,1:T(8,128)} fusion(f32[32,2,256,256]{3,2,0,1:T(8,128)} %get-tuple-element.149, bf16[32,2,256,256]{3,2,0,1:T(8,128)(2,1)} %pad_maximum_fusion.7, pred[]{:T(512)S(6)} %compare.4), kind=kLoop, calls=%fused_computation.clone.1 | loop fusion | flops 12582912 | bytes 41943040 | tf_op jit(solution)/shard_map/while/body/eval_jaxpr/add | solution.py:97
  243.9 1.3 fusion.87
  245.2 3.2 fusion.88
  248.4 6.3 %pad_maximum_fusion.7 = bf16[32,2,256,256]{3,2,0,1:T(8,128)(2,1)} fusion(bf16[32,1,256,256]{3,2,0,1:T(8,128)(2,1)S(1)} %fusion.87, bf16[32,1,256,256]{3,2,0,1:T(8,128)(2,1)} %fusion.88), kind=kLoop, calls=%fused_computation.1.clone.1 | loop fusion | flops 4194304 | bytes 16777216 | tf_op jit(solution)/shard_map/while/body/eval_jaxpr/stack | solution.py:95
  254.8 14.0 %select_add_fusion.2 = f32[32,2,256,256]{3,2,0,1:T(8,128)} fusion(f32[32,2,256,256]{3,2,0,1:T(8,128)} %get-tuple-element.149, bf16[32,2,256,256]{3,2,0,1:T(8,128)(2,1)} %pad_maximum_fusion.7, pred[]{:T(512)S(6)} %compare.4), kind=kLoop, calls=%fused_computation.clone.1 | loop fusion | flops 12582912 | bytes 41943040 | tf_op jit(solution)/shard_map/while/body/eval_jaxpr/add | solution.py:97
  268.9 1.3 fusion.87
  270.2 3.2 fusion.88
  273.5 6.3 %pad_maximum_fusion.7 = bf16[32,2,256,256]{3,2,0,1:T(8,128)(2,1)} fusion(bf16[32,1,256,256]{3,2,0,1:T(8,128)(2,1)S(1)} %fusion.87, bf16[32,1,256,256]{3,2,0,1:T(8,128)(2,1)} %fusion.88), kind=kLoop, calls=%fused_computation.1.clone.1 | loop fusion | flops 4194304 | bytes 16777216 | tf_op jit(solution)/shard_map/while/body/eval_jaxpr/stack | solution.py:95
  279.8 14.0 %select_add_fusion.2 = f32[32,2,256,256]{3,2,0,1:T(8,128)} fusion(f32[32,2,256,256]{3,2,0,1:T(8,128)} %get-tuple-element.149, bf16[32,2,256,256]{3,2,0,1:T(8,128)(2,1)} %pad_maximum_fusion.7, pred[]{:T(512)S(6)} %compare.4), kind=kLoop, calls=%fused_computation.clone.1 | loop fusion | flops 12582912 | bytes 41943040 | tf_op jit(solution)/shard_map/while/body/eval_jaxpr/add | solution.py:97
  294.0 1.3 fusion.87
  295.3 3.2 fusion.88
  298.6 6.3 %pad_maximum_fusion.7 = bf16[32,2,256,256]{3,2,0,1:T(8,128)(2,1)} fusion(bf16[32,1,256,256]{3,2,0,1:T(8,128)(2,1)S(1)} %fusion.87, bf16[32,1,256,256]{3,2,0,1:T(8,128)(2,1)} %fusion.88), kind=kLoop, calls=%fused_computation.1.clone.1 | loop fusion | flops 4194304 | bytes 16777216 | tf_op jit(solution)/shard_map/while/body/eval_jaxpr/stack | solution.py:95
  304.9 14.0 %select_add_fusion.2 = f32[32,2,256,256]{3,2,0,1:T(8,128)} fusion(f32[32,2,256,256]{3,2,0,1:T(8,128)} %get-tuple-element.149, bf16[32,2,256,256]{3,2,0,1:T(8,128)(2,1)} %pad_maximum_fusion.7, pred[]{:T(512)S(6)} %compare.4), kind=kLoop, calls=%fused_computation.clone.1 | loop fusion | flops 12582912 | bytes 41943040 | tf_op jit(solution)/shard_map/while/body/eval_jaxpr/add | solution.py:97
  318.9 11.7 %copy.35 = f32[32,2,256,256]{3,2,1,0:T(8,128)} copy(f32[32,2,256,256]{3,2,0,1:T(8,128)} %get-tuple-element.94) | data formatting | bytes 33554432
  (39 shorter events, 4.6 us)
Async XLA Ops:
  0.6 52.3 %copy-start = (bf16[16,32,2048]{2,1,0:T(8,128)(2,1)S(1)}, bf16[16,32,2048]{2,1,0:T(8,128)(2,1)}, u32[]{:S(2)}) copy-start(bf16[16,32,2048]{2,1,0:T(8,128)(2,1)} %param.5) | copy-start | bytes 6291460
  3.8 47.3 %collective-permute-start = (bf16[15,32,2048]{2,1,0:T(8,128)(2,1)}, bf16[15,32,2048]{2,1,0:T(8,128)(2,1)}, u32[]{:S(2)}, u32[]{:S(2)}) collective-permute-start(bf16[15,32,2048]{2,1,0:T(8,128)(2,1)} %slice.112), channel_id=1, source_target_pairs={{0,1},{1,2},{2,3},{4,5},{5,6},{6,7},{8,9},{9,10},{10,11},{12,13},{... | collective-permute-start | bytes 5898248 | tf_op jit(solution)/shard_map/ppermute | solution.py:11
  164.5 53.3 %all-to-all-start.1 = ((bf16[1,128,256,2,16]{2,4,3,0,1:T(8,128)(2,1)}), bf16[1,128,256,2,16]{2,4,3,0,1:T(8,128)(2,1)S(1)}, u32[]{:S(2)}, u32[]{:S(2)}) async-start(bf16[1,128,256,2,16]{2,4,3,0,1:T(8,128)(2,1)} %copy.30), calls=%async_computation.1 | async-start | bytes 4194304 | tf_op jit(solution)/shard_map/all_to_all | solution.py:71
  219.2 111.4 %all-to-all-start.2 = ((f32[4,1,512]{2,1,0:T(1,128)}), f32[4,1,512]{2,1,0:T(1,128)S(1)}, u32[]{:S(2)}, u32[]{:S(2)}) async-start(f32[4,1,512]{2,1,0:T(1,128)} %reshape.90), calls=%async_computation.2 | async-start | bytes 16384 | tf_op jit(solution)/shard_map/all_to_all | solution.py:89
